TPU v7x, 32 devices: a whole 2x2x4 slice. The times are simulated.
32 devices in a mesh: batch: 4 (over z), seq: 2 (over core), ch: 4 (over y, x).
Axes of the slice: x: 2, y: 2, z: 4, core: 2. Of those that a mesh axis runs over, the one named last changes fastest.
Arguments:
- inputs: bfloat16 [16, 1280, 2048], P('batch', 'ch', 'seq'), may hold values from -6 to 6
- segment_ids: int32 [16, 2048], P('batch', 'seq'), may hold values from 0 to 7, never falling along the last dimension, each value on 1 to 512 neighbouring positions
- norm0_gain: float32 [1280], P('ch'), may hold values from 0.1 to 1.9
- norm0_shift: float32 [1280], P('ch'), may hold values from -3 to 3
- w_inner: bfloat16 [1280, 640], P('ch'), may hold values from -0.15625 to 0.15625
- b_inner: float32 [640], P('ch'), may hold values from -3 to 3
- norm1_gain: float32 [640], P('ch'), may hold values from 0.1 to 1.9
- norm1_shift: float32 [640], P('ch'), may hold values from -3 to 3
- w_conv: bfloat16 [5, 640, 640], P(None, 'ch'), may hold values from -0.109375 to 0.109375
- b_conv: float32 [640], P('ch'), may hold values from -3 to 3
- norm2_gain: float32 [640], P('ch'), may hold values from 0.1 to 1.9
- norm2_shift: float32 [640], P('ch'), may hold values from -3 to 3
- w_outer: bfloat16 [640, 1280], P('ch'), may hold values from -0.25 to 0.25
- b_outer: float32 [1280], P('ch'), may hold values from -3 to 3
- cotangent: bfloat16 [16, 1280, 2048], P('batch', 'ch', 'seq'), may hold values from -6 to 6
Outputs:
- output: bfloat16 [16, 1280, 2048], P('batch', 'ch', 'seq')
- input_grad: bfloat16 [16, 1280, 2048], P('batch', 'ch', 'seq')
- grad_norm0_gain: float32 [1280], P('ch')
- grad_norm0_shift: float32 [1280], P('ch')
- grad_w_inner: float32 [1280, 640], P('ch')
- grad_b_inner: float32 [640], P('ch')
- grad_norm1_gain: float32 [640], P('ch')
- grad_norm1_shift: float32 [640], P('ch')
- grad_w_conv: float32 [5, 640, 640], P(None, 'ch')
- grad_b_conv: float32 [640], P('ch')
- grad_norm2_gain: float32 [640], P('ch')
- grad_norm2_shift: float32 [640], P('ch')
- grad_w_outer: float32 [640, 1280], P('ch')
- grad_b_outer: float32 [1280], P('ch')
Inputs may be any that keep to these rules, and one draw needn't show every extreme that they name: `segment_ids`: along a row the ids never fall; each protein is one run of 1 to 512 residues, one run of each row has exactly 512, and every row holds all 8 ids.
All inputs are finite; a program needn't handle non-finite values.
Results may differ from a plain program's by a relative error of at most 0.0065.
Values may be sent and summed in bfloat16 or wider, within the bound.
A program may use at most 192 MiB of HBM per device.

v0:
```python
import jax
import jax.numpy as jnp
from jax import lax
from jax.sharding import PartitionSpec as P

KERNEL_TAPS = 5
DILATION_SPACING = 32
EPSILON = 1e-05


def extended(x, sides, width):
    for axis, dim in sides:
        size, length = (lax.axis_size(axis), x.shape[dim])
        up = [(i, (i + 1) % size) for i in range(size - 1)]
        down = [(j, i) for i, j in up]
        last = lax.slice_in_dim(x, length - width, length, axis=dim)
        leading = lax.slice_in_dim(x, 0, width, axis=dim)
        before = lax.ppermute(last, axis, up)
        after = lax.ppermute(leading, axis, down)
        x = jnp.concatenate([before, x, after], axis=dim)
    return x


def gelu_exact(values):
    return jax.nn.gelu(values, approximate=False)


def gelu_back(point, grad):
    return jax.vjp(gelu_exact, point)[1](grad)[0]


def channel_sums(first, second):
    return lax.psum((first, second), "ch")


def normalize(values, gain, shift):
    width = values.shape[1] * lax.axis_size("ch")
    total, squares = channel_sums(
        jnp.sum(values, axis=1, keepdims=True), jnp.sum(values * values, axis=1, keepdims=True)
    )
    center = total / width
    spread = squares / width - center * center
    scale = lax.rsqrt(spread + EPSILON)
    unit = (values - center) * scale
    return (unit * gain[:, None] + shift[:, None], unit, scale)


def normalize_back(grad, unit, scale, gain):
    width = grad.shape[1] * lax.axis_size("ch")
    scaled = grad * gain[:, None]
    first, second = channel_sums(
        jnp.sum(scaled, axis=1, keepdims=True), jnp.sum(scaled * unit, axis=1, keepdims=True)
    )
    return scale * (scaled - first / width - unit * (second / width))


def shifted_taps(wide, wide_ids, own_ids, tap_displacements, border_extent):
    length = own_ids.shape[1]
    pieces = []
    for tap_displacement in tap_displacements:
        lower = border_extent + tap_displacement
        shifted = wide[:, :, lower : lower + length]
        matching = wide_ids[:, lower : lower + length] == own_ids
        pieces.append(jnp.where(matching[:, None, :], shifted, jnp.zeros_like(shifted)))
    return jnp.stack(pieces, axis=1)


def local(
    inputs,
    segment_ids,
    norm0_gain,
    norm0_shift,
    w_inner,
    b_inner,
    norm1_gain,
    norm1_shift,
    w_conv,
    b_conv,
    norm2_gain,
    norm2_shift,
    w_outer,
    b_outer,
    cotangent,
):
    border_extent = 2 * DILATION_SPACING
    tap_displacements = [
        (tap_stride - KERNEL_TAPS // 2) * DILATION_SPACING for tap_stride in range(KERNEL_TAPS)
    ]
    back_offsets = [-tap_displacement for tap_displacement in tap_displacements]
    residual = inputs.astype(jnp.float32)
    normed0, unit0, scale0 = normalize(residual, norm0_gain, norm0_shift)
    hidden0 = gelu_exact(normed0).astype(jnp.bfloat16)
    inner_terms = jnp.einsum("sdl,dh->shl", hidden0, w_inner, preferred_element_type=jnp.float32)
    inner = lax.psum_scatter(inner_terms, "ch", scatter_dimension=1, tiled=True) + b_inner[:, None]
    normed1, unit1, scale1 = normalize(inner, norm1_gain, norm1_shift)
    hidden1 = gelu_exact(normed1).astype(jnp.bfloat16)
    own_ids = segment_ids + 1
    wide_ids = extended(own_ids, (("seq", 1),), border_extent)
    wide_hidden = extended(hidden1, (("seq", 2),), border_extent)
    taps = shifted_taps(wide_hidden, wide_ids, own_ids, tap_displacements, border_extent)
    seqs, width, length = hidden1.shape
    taps_flat = taps.reshape(seqs, KERNEL_TAPS * width, length)
    kernel_flat = w_conv.reshape(KERNEL_TAPS * width, w_conv.shape[2])
    conv_terms = jnp.einsum(
        "scl,ch->shl", taps_flat, kernel_flat, preferred_element_type=jnp.float32
    )
    mixed = lax.psum_scatter(conv_terms, "ch", scatter_dimension=1, tiled=True) + b_conv[:, None]
    normed2, unit2, scale2 = normalize(mixed, norm2_gain, norm2_shift)
    hidden2 = gelu_exact(normed2).astype(jnp.bfloat16)
    outer_terms = jnp.einsum("shl,hd->sdl", hidden2, w_outer, preferred_element_type=jnp.float32)
    branch = lax.psum_scatter(outer_terms, "ch", scatter_dimension=1, tiled=True)
    output = (residual + branch + b_outer[:, None]).astype(jnp.bfloat16)
    piece = lax.all_gather(cotangent, "ch", axis=1, tiled=True)
    block = w_outer
    hidden_gradient = jnp.einsum("snl,hn->shl", piece, block, preferred_element_type=jnp.float32)
    part = jnp.einsum("shl,snl->hn", hidden2, piece, preferred_element_type=jnp.float32)
    grad_weight = part
    grad_hidden2 = hidden_gradient
    grad_w_outer = grad_weight
    grad_b_outer = jnp.sum(cotangent.astype(jnp.float32), axis=(0, 2))
    grad_normed2 = gelu_back(normed2, grad_hidden2)
    grad_norm2_gain = jnp.sum(grad_normed2 * unit2, axis=(0, 2))
    grad_norm2_shift = jnp.sum(grad_normed2, axis=(0, 2))
    grad_mixed = normalize_back(grad_normed2, unit2, scale2, norm2_gain).astype(jnp.bfloat16)
    grad_b_conv = jnp.sum(grad_mixed.astype(jnp.float32), axis=(0, 2))
    wide_grad = extended(grad_mixed, (("seq", 2),), border_extent)
    piece = lax.all_gather(wide_grad, "ch", axis=1, tiled=True)
    count = piece.shape[1]
    back_taps = shifted_taps(piece, wide_ids, own_ids, back_offsets, border_extent)
    back_flat = back_taps.reshape(seqs, KERNEL_TAPS * count, length)
    kernel_back = jnp.transpose(w_conv, (0, 2, 1)).reshape(KERNEL_TAPS * count, width)
    hidden_gradient = jnp.einsum(
        "sml,mc->scl", back_flat, kernel_back, preferred_element_type=jnp.float32
    )
    center = piece[:, :, border_extent : border_extent + length]
    part = jnp.einsum("sml,snl->mn", taps_flat, center, preferred_element_type=jnp.float32).reshape(
        KERNEL_TAPS, width, count
    )
    grad_kernel = part
    grad_hidden1 = hidden_gradient
    grad_normed1 = gelu_back(normed1, grad_hidden1)
    grad_norm1_gain = jnp.sum(grad_normed1 * unit1, axis=(0, 2))
    grad_norm1_shift = jnp.sum(grad_normed1, axis=(0, 2))
    grad_inner = normalize_back(grad_normed1, unit1, scale1, norm1_gain).astype(jnp.bfloat16)
    grad_b_inner = jnp.sum(grad_inner.astype(jnp.float32), axis=(0, 2))
    piece = lax.all_gather(grad_inner, "ch", axis=1, tiled=True)
    block = w_inner
    hidden_gradient = jnp.einsum("snl,dn->sdl", piece, block, preferred_element_type=jnp.float32)
    part = jnp.einsum("sdl,snl->dn", hidden0, piece, preferred_element_type=jnp.float32)
    grad_weight = part
    grad_normed0 = gelu_back(normed0, hidden_gradient)
    grad_norm0_gain = jnp.sum(grad_normed0 * unit0, axis=(0, 2))
    grad_norm0_shift = jnp.sum(grad_normed0, axis=(0, 2))
    input_grad = (
        cotangent.astype(jnp.float32) + normalize_back(grad_normed0, unit0, scale0, norm0_gain)
    ).astype(jnp.bfloat16)
    totals = lax.psum(
        (
            grad_norm0_gain,
            grad_norm0_shift,
            grad_weight,
            grad_b_inner,
            grad_norm1_gain,
            grad_norm1_shift,
            grad_kernel,
            grad_b_conv,
            grad_norm2_gain,
            grad_norm2_shift,
            grad_w_outer,
            grad_b_outer,
        ),
        ("batch", "seq"),
    )
    return (
        output,
        input_grad,
        totals[0],
        totals[1],
        totals[2],
        totals[3],
        totals[4],
        totals[5],
        totals[6],
        totals[7],
        totals[8],
        totals[9],
        totals[10],
        totals[11],
    )


def solution(mesh):
    return jax.shard_map(
        local,
        mesh=mesh,
        in_specs=(
            P("batch", "ch", "seq"),
            P("batch", "seq"),
            P("ch"),
            P("ch"),
            P("ch", None),
            P("ch"),
            P("ch"),
            P("ch"),
            P(None, "ch", None),
            P("ch"),
            P("ch"),
            P("ch"),
            P("ch", None),
            P("ch"),
            P("batch", "ch", "seq"),
        ),
        out_specs=(
            P("batch", "ch", "seq"),
            P("batch", "ch", "seq"),
            P("ch"),
            P("ch"),
            P("ch", None),
            P("ch"),
            P("ch"),
            P("ch"),
            P(None, "ch", None),
            P("ch"),
            P("ch"),
            P("ch"),
            P("ch", None),
            P("ch"),
        ),
        check_vma=False,
    )
```

profile of v0, /device:TPU:0, one launch (start us, length us, event | category | flops | bytes accessed | tf_op | source)
XLA Modules:
  0.0 1400.8 jit_solution(3146654529673238040)
XLA Ops:
  9.8 17.8 %all-reduce.10 = (f32[4,1,1024]{2,0,1:T(4,128)S(1)}, f32[4,1,1024]{2,0,1:T(4,128)S(1)}) all-reduce(f32[4,1,1024]{2,0,1:T(4,128)S(1)} %bitcast.197, f32[4,1,1024]{2,0,1:T(4,128)S(1)} %bitcast.196), channel_id=1, replica_groups=mesh['batch'=4,'seq'=2,'ch'=4] {'ch'}, use_global_device_ids=true, to_apply=%region_3.0 | all-reduce | flops 8192 | bytes 65536 | tf_op jit(solution)/shard_map/psum | solution.py:33
  27.7 14.6 %multiply_convert_fusion = (bf16[4,320,1024]{2,1,0:T(8,128)(2,1)S(1)}, f32[4,320,1024]{2,1,0:T(8,128)}) fusion(bf16[4,320,1024]{2,1,0:T(8,128)(2,1)} %param.15, f32[320]{0:T(512)S(1)} %copy-done.34, f32[320]{0:T(512)S(1)} %copy-done.28, f32[4,1024]{1,0:T(4,128)S(1)} %get-tuple-element.117, f32[4,1024]{1,0:T(4,128)S(1)} %get-tuple-element.116), kind=kLoop, calls=%fused_computation.51 | loop fusion | flops 91750400 | bytes 10521088 | tf_op jit(solution)/shard_map/convert_element_type | solution.py:92
  49.6 12.9 copy.63
  68.8 199.4 %all-reduce.16.cloned.1.call-done = f32[4,640,1024]{2,0,1:T(4,128)} async-done(((f32[4,640,1024]{2,0,1:T(4,128)}), f32[4,640,1024]{2,0,1:T(4,128)}) %all-reduce.16.cloned.1.call-update) | async-done | bytes 10485776
  273.6 15.7 %all-reduce.9 = (f32[4,1,1024]{2,0,1:T(4,128)S(1)}, f32[4,1,1024]{2,0,1:T(4,128)S(1)}) all-reduce(f32[4,1,1024]{2,0,1:T(4,128)S(1)} %bitcast.193, f32[4,1,1024]{2,0,1:T(4,128)S(1)} %bitcast.192), channel_id=1, replica_groups=mesh['batch'=4,'seq'=2,'ch'=4] {'ch'}, use_global_device_ids=true, to_apply=%region_8.0 | all-reduce | flops 8192 | bytes 65536 | tf_op jit(solution)/shard_map/psum | solution.py:33
  313.8 9.1 convolution_bitcast_fusion.2
  322.9 12.9 copy.65
  336.6 206.1 %all-reduce.18.cloned.1.call-done = f32[4,640,1024]{2,0,1:T(4,128)} async-done(((f32[4,640,1024]{2,0,1:T(4,128)}), f32[4,640,1024]{2,0,1:T(4,128)}) %all-reduce.18.cloned.1.call-update) | async-done | bytes 10485776
  547.9 16.7 %all-reduce.8 = (f32[4,1,1024]{2,0,1:T(4,128)S(1)}, f32[4,1,1024]{2,0,1:T(4,128)S(1)}) all-reduce(f32[4,1,1024]{2,0,1:T(4,128)S(1)} %bitcast.195, f32[4,1,1024]{2,0,1:T(4,128)S(1)} %bitcast.194), channel_id=1, replica_groups=mesh['batch'=4,'seq'=2,'ch'=4] {'ch'}, use_global_device_ids=true, to_apply=%region_13.14 | all-reduce | flops 8192 | bytes 65536 | tf_op jit(solution)/shard_map/psum | solution.py:33
  573.8 76.4 %all-gather.4.cloned.1.call-done = bf16[4,1280,1024]{2,1,0:T(8,128)(2,1)} async-done(((bf16[4,320,1024]{2,1,0:T(8,128)(2,1)}), bf16[4,1280,1024]{2,1,0:T(8,128)(2,1)}) %all-gather.4.cloned.1.call-update) | async-done | bytes 10485776 | tf_op jit(solution)/shard_map/all_gather | solution.py:113
  650.2 12.3 multiply_reduce_fusion.1
  662.5 15.3 %all-reduce.7 = (f32[4,1,1024]{2,0,1:T(4,128)S(1)}, f32[4,1,1024]{2,0,1:T(4,128)S(1)}) all-reduce(f32[4,1,1024]{2,0,1:T(4,128)S(1)} %bitcast.200, f32[4,1,1024]{2,0,1:T(4,128)S(1)} %bitcast.201), channel_id=1, replica_groups=mesh['batch'=4,'seq'=2,'ch'=4] {'ch'}, use_global_device_ids=true, to_apply=%region_18.19 | all-reduce | flops 8192 | bytes 65536 | tf_op jit(solution)/shard_map/psum | solution.py:33
  694.9 66.8 %all-gather.6.cloned.1.call-done = bf16[4,640,1152]{2,0,1:T(4,128)(2,1)} async-done(((bf16[4,160,1152]{2,0,1:T(4,128)(2,1)}), bf16[4,640,1152]{2,0,1:T(4,128)(2,1)}) %all-gather.6.cloned.1.call-update) | async-done | bytes 5898256 | tf_op jit(solution)/shard_map/all_gather | solution.py:127
  761.7 25.3 %fusion.110 = (bf16[4,640,1024]{2,0,1:T(4,128)(2,1)S(1)}, bf16[4,640,1024]{2,0,1:T(4,128)(2,1)S(1)}, bf16[4,640,1024]{2,0,1:T(4,128)(2,1)S(1)}, bf16[4,640,1024]{2,0,1:T(4,128)(2,1)S(1)}, bf16[4,640,1024]{2,0,1:T(4,128)(2,1)}) fusion(bf16[4,640,1152]{2,0,1:T(4,128)(2,1)} %all-gather.6.cloned.1.call-done), kind=kLoop, calls=%fused_computation.198 | loop fusion | bytes 52428800 | tf_op jit(solution)/shard_map/slice | solution.py:62
  812.6 18.1 %multiply_reduce_fusion.2 = (f32[160]{0:T(256)S(1)}, f32[4,1024]{1,0:T(4,128)S(1)}, f32[4,1024]{1,0:T(4,128)S(1)}, f32[160]{0:T(256)S(1)}, f32[4,160,1024]{2,1,0:T(8,128)}) fusion(f32[4,1024]{1,0:T(4,128)S(1)} %get-tuple-element.115, f32[4,1024]{1,0:T(4,128)S(1)} %get-tuple-element.114, f32[160]{0:T(256)S(1)} %copy-done.24, ...), kind=kOutput, calls=%fused_computation.96 | convolution fusion | flops 4248690176 | bytes 32550016 | tf_op jit(solution)/shard_map/sml,mc->scl/dot_general | solution.py:132
  830.8 15.4 %all-reduce.6 = (f32[4,1,1024]{2,0,1:T(4,128)S(1)}, f32[4,1,1024]{2,0,1:T(4,128)S(1)}) all-reduce(f32[4,1,1024]{2,0,1:T(4,128)S(1)} %bitcast.202, f32[4,1,1024]{2,0,1:T(4,128)S(1)} %bitcast.203), channel_id=1, replica_groups=mesh['batch'=4,'seq'=2,'ch'=4] {'ch'}, use_global_device_ids=true, to_apply=%region_22.23 | all-reduce | flops 8192 | bytes 65536 | tf_op jit(solution)/shard_map/psum | solution.py:33
  853.2 9.4 convolution_bitcast_fusion
  862.6 25.4 %copy.67 = f32[4,1280,1024]{2,0,1:T(4,128)} copy(f32[4,1280,1024]{1,2,0:T(8,128)} %convolution_bitcast_fusion) | data formatting | bytes 41943040 | tf_op jit(solution)/shard_map/shl,hd->sdl/transpose | solution.py:110
  897.4 12.0 fusion.74
  923.9 12.3 fusion.17
  936.2 17.4 %all-reduce.5 = (f32[4,1,1024]{2,0,1:T(4,128)S(1)}, f32[4,1,1024]{2,0,1:T(4,128)S(1)}) all-reduce(f32[4,1,1024]{2,0,1:T(4,128)S(1)} %bitcast.198, f32[4,1,1024]{2,0,1:T(4,128)S(1)} %bitcast.199), channel_id=1, replica_groups=mesh['batch'=4,'seq'=2,'ch'=4] {'ch'}, use_global_device_ids=true, to_apply=%region_26.27 | all-reduce | flops 8192 | bytes 65536 | tf_op jit(solution)/shard_map/psum | solution.py:33
  953.7 340.3 %all-reduce.20.cloned.1.call-done = f32[4,1280,1024]{2,0,1:T(4,128)} async-done(((f32[4,1280,1024]{2,0,1:T(4,128)}), f32[4,1280,1024]{2,0,1:T(4,128)}) %all-reduce.20.cloned.1.call-update) | async-done | bytes 20971536
  1306.6 30.6 %all-reduce.3 = (f32[320]{0:T(512)}, f32[320]{0:T(512)}, f32[160]{0:T(256)}, f32[160]{0:T(256)}, f32[160]{0:T(256)}, /*index=5*/f32[160]{0:T(256)}, f32[160]{0:T(256)}, f32[160]{0:T(256)}, f32[320]{0:T(512)}) all-reduce(f32[320]{0:T(512)S(1)} %get-tuple-element.42, ...), channel_id=1, replica_groups=mesh['batch'=4,'seq'=2,'ch'=4] {'batch','seq'}, use_global_device_ids=true, to_apply=%region_28.29 | all-reduce | flops 1920 | bytes 15360 | tf_op jit(solution)/shard_map/psum | solution.py:157
  1337.2 50.5 %all-reduce.22.cloned.1.call-done = (f32[320,640]{1,0:T(8,128)}, f32[5,160,640]{2,1,0:T(8,128)}, f32[160,1280]{1,0:T(8,128)}) async-done(((f32[320,640]{1,0:T(8,128)}, f32[5,160,640]{2,1,0:T(8,128)}, f32[160,1280]{1,0:T(8,128)}), (f32[320,640]{1,0:T(8,128)}, f32[5,160,640]{2,1,0:T(8,128)}, f32[160,1280]{1,0:T(8,128)})) %all-reduce.22.cloned.1.call-update) | async-done | bytes 3686416 | tf_op jit(solution)/shard_map/psum | solution.py:157
  (153 shorter events, 151.9 us)
Async XLA Ops:
  7.2 306.6 %copy-start = (bf16[5,160,640]{2,1,0:T(8,128)(2,1)S(1)}, bf16[5,160,640]{2,1,0:T(8,128)(2,1)}, u32[]{:S(2)}) copy-start(bf16[5,160,640]{2,1,0:T(8,128)(2,1)} %param.23) | copy-start | bytes 3072004
  7.2 20.4 %copy-start.28 = (f32[320]{0:T(512)S(1)}, f32[320]{0:T(512)}, u32[]{:S(2)}) copy-start(f32[320]{0:T(512)} %param.17) | copy-start | bytes 3844
  7.2 20.4 %copy-start.34 = (f32[320]{0:T(512)S(1)}, f32[320]{0:T(512)}, u32[]{:S(2)}) copy-start(f32[320]{0:T(512)} %param.18) | copy-start | bytes 3844
  7.2 261.1 %all-reduce.16.cloned.1.call-start = ((), (), s32[]{:S(2)}) async-start(), calls=%async_computation.3 | async-start | bytes 20971520
  62.5 480.2 %all-reduce.18.cloned.1.call-start = ((), (), s32[]{:S(2)}) async-start(), calls=%async_computation.4 | async-start | bytes 20971520
  63.2 235.7 %collective-permute-start.2 = (s32[4,64]{1,0:T(4,128)S(1)}, s32[4,64]{1,0:T(4,128)S(1)}, u32[]{:S(2)}, u32[]{:S(2)}) collective-permute-start(s32[4,64]{1,0:T(4,128)S(1)} %get-tuple-element.112), channel_id=1, source_target_pairs={{4,0},{5,1},{6,2},{7,3},{12,8},{13,9},{14,10},{15,11},{20,16},{21,... | collective-permute-start | bytes 3080 | tf_op jit(solution)/shard_map/ppermute | solution.py:19
  64.5 234.4 %collective-permute-start = (s32[4,64]{1,0:T(4,128)S(1)}, s32[4,64]{1,0:T(4,128)S(1)}, u32[]{:S(2)}, u32[]{:S(2)}) collective-permute-start(s32[4,64]{1,0:T(4,128)S(1)} %get-tuple-element.113), channel_id=1, source_target_pairs={{0,4},{1,5},{2,6},{3,7},{8,12},{9,13},{10,14},{11,15},{16,20},{17,... | collective-permute-start | bytes 3080 | tf_op jit(solution)/shard_map/ppermute | solution.py:18
  68.8 203.3 %copy-start.23 = (f32[160]{0:T(256)S(1)}, f32[160]{0:T(256)}, u32[]{:S(2)}) copy-start(f32[160]{0:T(256)} %param.20) | copy-start | bytes 1924
  272.1 17.2 %copy-start.26 = (f32[160]{0:T(256)S(1)}, f32[160]{0:T(256)}, u32[]{:S(2)}) copy-start(f32[160]{0:T(256)} %param.21) | copy-start | bytes 1924
  272.1 17.2 %copy-start.32 = (f32[160]{0:T(256)S(1)}, f32[160]{0:T(256)}, u32[]{:S(2)}) copy-start(f32[160]{0:T(256)} %param.22) | copy-start | bytes 1924
  297.6 2.9 collective-permute-start.1
  299.0 10.4 collective-permute-start.3
  335.8 314.4 %all-gather.4.cloned.1.call-start = ((), (), s32[]{:S(2)}) async-start(), calls=%async_computation | async-start | bytes 13107200 | tf_op jit(solution)/shard_map/all_gather | solution.py:113
  336.5 209.9 %copy-start.25 = (f32[160]{0:T(256)S(1)}, f32[160]{0:T(256)}, u32[]{:S(2)}) copy-start(f32[160]{0:T(256)} %param.24) | copy-start | bytes 1924
  336.5 425.2 %all-gather.6.cloned.1.call-start = ((), (), s32[]{:S(2)}) async-start(), calls=%async_computation.1 | async-start | bytes 7372800 | tf_op jit(solution)/shard_map/all_gather | solution.py:127
  546.4 18.2 %copy-start.30 = (f32[160]{0:T(256)S(1)}, f32[160]{0:T(256)}, u32[]{:S(2)}) copy-start(f32[160]{0:T(256)} %param.25) | copy-start | bytes 1924
  546.4 18.2 %copy-start.37 = (f32[160]{0:T(256)S(1)}, f32[160]{0:T(256)}, u32[]{:S(2)}) copy-start(f32[160]{0:T(256)} %param.26) | copy-start | bytes 1924
  564.7 85.5 %copy-start.13 = (bf16[160,1280]{1,0:T(8,128)(2,1)S(1)}, bf16[160,1280]{1,0:T(8,128)(2,1)}, u32[]{:S(2)}) copy-start(bf16[160,1280]{1,0:T(8,128)(2,1)} %param.27) | copy-start | bytes 1228804
  683.5 4.4 collective-permute-start.5
  684.8 4.1 collective-permute-start.4
  694.6 220.1 %all-gather.8.cloned.1.call-start = ((), (), s32[]{:S(2)}) async-start(), calls=%async_computation.2 | async-start | bytes 6553600 | tf_op jit(solution)/shard_map/all_gather | solution.py:146
  853.1 440.9 %all-reduce.20.cloned.1.call-start = ((), (), s32[]{:S(2)}) async-start(), calls=%async_computation.5 | async-start | bytes 41943040
  888.0 499.6 %all-reduce.22.cloned.1.call-start = ((), (), s32[]{:S(2)}) async-start(), calls=%async_computation.6 | async-start | bytes 7372800 | tf_op jit(solution)/shard_map/psum | solution.py:157
  953.7 344.3 %copy-start.36 = (f32[320]{0:T(512)S(1)}, f32[320]{0:T(512)}, u32[]{:S(2)}) copy-start(f32[320]{0:T(512)} %param.28) | copy-start | bytes 3844
  (30 other events, 146.3 us)
Sparse Core Ops, SparseCore 0:
  62.6 205.6 all-reduce.15
  335.9 206.6 all-reduce.17
  544.5 105.6 all-gather.3
  694.8 66.8 all-gather.5
  853.3 61.3 all-gather.7
  918.1 375.9 all-reduce.19
  1297.9 89.6 all-reduce.21
where the time goes:
time: 1410 us; the launch traced here: 1400 us
  waiting for transfers between devices  947 us (67%)
  blocking collectives  129 us (9%)
  local copies, waits for them, and re-layouts  115 us (8%)
  matrix products  95.6 us (7%)
  other arithmetic  86.6 us (6%)
  between operations  16.2 us (1%)
    unnamed x10, waiting for transfers between devices  747 us
    psum x6, blocking collectives, channel_sums(): return lax.psum((first, second), 'ch')  98.3 us
    all_gather x1, waiting for transfers between devices, local(): piece = lax.all_gather(cotangent, 'ch', axis=1, tiled=True)  76.4 us
    all_gather x1, waiting for transfers between devices, local(): piece = lax.all_gather(wide_grad, 'ch', axis=1, tiled=True)  66.8 us
    psum x1, waiting for transfers between devices, local(): lax.psum((grad_norm0_gain, grad_norm0_shift, grad_weight, grad_b_inner, g...  50.5 us
    psum x1, blocking collectives, local(): lax.psum((grad_norm0_gain, grad_norm0_shift, grad_weight, grad_b_inner, g...  30.6 us
    unnamed x90, local copies, waits for them, and re-layouts  30.3 us
  transfers between devices with their start and end apart: 13, of which 8 were waited for; matrix products, arithmetic and copies ran while one was open for 9% of the time, Pallas kernels for 0%

commit v1 on v0

--- a/solution.py
+++ b/solution.py
@@ -1,3 +1,4 @@
+import functools
 import jax
 import jax.numpy as jnp
 from jax import lax
@@ -6,6 +7,14 @@
 KERNEL_TAPS = 5
 DILATION_SPACING = 32
 EPSILON = 1e-05
+
+
+def match_corner_by_axis(own_rows, group_axis, lane_axis):
+    prior = lax.psum(own_rows, group_axis)
+    return lax.psum(prior, lane_axis)
+
+
+leaves_number = functools.partial(match_corner_by_axis, group_axis="seq", lane_axis="batch")
 
 
 def extended(x, sides, width):
@@ -154,7 +163,7 @@
     input_grad = (
         cotangent.astype(jnp.float32) + normalize_back(grad_normed0, unit0, scale0, norm0_gain)
     ).astype(jnp.bfloat16)
-    totals = lax.psum(
+    totals = leaves_number(
         (
             grad_norm0_gain,
             grad_norm0_shift,
@@ -168,8 +177,7 @@
             grad_norm2_shift,
             grad_w_outer,
             grad_b_outer,
-        ),
-        ("batch", "seq"),
+        )
     )
     return (
         output,

time: 1410 us -> 1500 us (1.064)
  waiting for transfers between devices: 947 us -> 1050 us
    psum x1 -> x2, waiting for transfers between devices: 50.5 us -> 107 us  [the longest x1 107 us: match_corner_by_axis(): return lax.psum(prior, lane_axis)]
    all_gather x1, waiting for transfers between devices: 5.33 us -> 41.7 us  [local(): piece = lax.all_gather(grad_inner, 'ch', axis=1, tiled=True)]
    psum x1 -> x2, blocking collectives: 30.6 us -> 23.7 us  [the longest x1 20.4 us: match_corner_by_axis(): return lax.psum(prior, lane_axis)]
    unnamed x10 -> x11, waiting for transfers between devices: 747 us -> 753 us
    unnamed x90 -> x94, local copies, waits for them, and re-layouts: 30.3 us -> 30.1 us
  transfers between devices with their start and end apart: 13 -> 14, of which waited for: 8 -> 8; matrix products, arithmetic and copies ran while one was open for 9% -> 8% of each run, Pallas kernels for 0% -> 0%
where the time goes in v1:
time: 1500 us; the launch traced here: 1490 us
  waiting for transfers between devices  1050 us (70%)
  blocking collectives  121 us (8%)
  local copies, waits for them, and re-layouts  115 us (8%)
  matrix products  95.1 us (6%)
  other arithmetic  86.6 us (6%)
  between operations  16.3 us (1%)
    unnamed x11, waiting for transfers between devices  753 us
    psum x1, waiting for transfers between devices, match_corner_by_axis(): return lax.psum(prior, lane_axis)  107 us
    psum x6, blocking collectives, channel_sums(): return lax.psum((first, second), 'ch')  96.9 us
    all_gather x1, waiting for transfers between devices, local(): piece = lax.all_gather(cotangent, 'ch', axis=1, tiled=True)  76.8 us
    all_gather x1, waiting for transfers between devices, local(): piece = lax.all_gather(wide_grad, 'ch', axis=1, tiled=True)  66.8 us
    all_gather x1, waiting for transfers between devices, local(): piece = lax.all_gather(grad_inner, 'ch', axis=1, tiled=True)  41.7 us
    unnamed x94, local copies, waits for them, and re-layouts  30.1 us
  transfers between devices with their start and end apart: 14, of which 8 were waited for; matrix products, arithmetic and copies ran while one was open for 8% of the time, Pallas kernels for 0%

profile of v1, /device:TPU:0, one launch (start us, length us, event | category | flops | bytes accessed | tf_op | source)
XLA Modules:
  0.0 1492.0 jit_solution(13114289917320067908)
XLA Ops:
  9.8 17.8 %all-reduce.8 = (f32[4,1,1024]{2,0,1:T(4,128)S(1)}, f32[4,1,1024]{2,0,1:T(4,128)S(1)}) all-reduce(f32[4,1,1024]{2,0,1:T(4,128)S(1)} %bitcast.199, f32[4,1,1024]{2,0,1:T(4,128)S(1)} %bitcast.198), channel_id=1, replica_groups=mesh['batch'=4,'seq'=2,'ch'=4] {'ch'}, use_global_device_ids=true, to_apply=%region_3.0 | all-reduce | flops 8192 | bytes 65536 | tf_op jit(solution)/shard_map/psum | solution.py:42
  27.7 14.6 multiply_convert_fusion
  49.5 12.9 copy.63
  68.8 199.5 %all-reduce.19.cloned.1.call-done = f32[4,640,1024]{2,0,1:T(4,128)} async-done(((f32[4,640,1024]{2,0,1:T(4,128)}), f32[4,640,1024]{2,0,1:T(4,128)}) %all-reduce.19.cloned.1.call-update) | async-done | bytes 10485776
  273.5 15.7 %all-reduce.7 = (f32[4,1,1024]{2,0,1:T(4,128)S(1)}, f32[4,1,1024]{2,0,1:T(4,128)S(1)}) all-reduce(f32[4,1,1024]{2,0,1:T(4,128)S(1)} %bitcast.195, f32[4,1,1024]{2,0,1:T(4,128)S(1)} %bitcast.194), channel_id=1, replica_groups=mesh['batch'=4,'seq'=2,'ch'=4] {'ch'}, use_global_device_ids=true, to_apply=%region_8.0 | all-reduce | flops 8192 | bytes 65536 | tf_op jit(solution)/shard_map/psum | solution.py:42
  323.2 12.9 copy.65
  336.9 206.1 %all-reduce.21.cloned.1.call-done = f32[4,640,1024]{2,0,1:T(4,128)} async-done(((f32[4,640,1024]{2,0,1:T(4,128)}), f32[4,640,1024]{2,0,1:T(4,128)}) %all-reduce.21.cloned.1.call-update) | async-done | bytes 10485776
  548.2 16.4 %all-reduce.6 = (f32[4,1,1024]{2,0,1:T(4,128)S(1)}, f32[4,1,1024]{2,0,1:T(4,128)S(1)}) all-reduce(f32[4,1,1024]{2,0,1:T(4,128)S(1)} %bitcast.197, f32[4,1,1024]{2,0,1:T(4,128)S(1)} %bitcast.196), channel_id=1, replica_groups=mesh['batch'=4,'seq'=2,'ch'=4] {'ch'}, use_global_device_ids=true, to_apply=%region_13.14 | all-reduce | flops 8192 | bytes 65536 | tf_op jit(solution)/shard_map/psum | solution.py:42
  573.8 76.8 %all-gather.4.cloned.1.call-done = bf16[4,1280,1024]{2,1,0:T(8,128)(2,1)} async-done(((bf16[4,320,1024]{2,1,0:T(8,128)(2,1)}), bf16[4,1280,1024]{2,1,0:T(8,128)(2,1)}) %all-gather.4.cloned.1.call-update) | async-done | bytes 10485776 | tf_op jit(solution)/shard_map/all_gather | solution.py:122
  650.5 12.3 multiply_reduce_fusion.1
  662.8 15.4 %all-reduce.5 = (f32[4,1,1024]{2,0,1:T(4,128)S(1)}, f32[4,1,1024]{2,0,1:T(4,128)S(1)}) all-reduce(f32[4,1,1024]{2,0,1:T(4,128)S(1)} %bitcast.202, f32[4,1,1024]{2,0,1:T(4,128)S(1)} %bitcast.203), channel_id=1, replica_groups=mesh['batch'=4,'seq'=2,'ch'=4] {'ch'}, use_global_device_ids=true, to_apply=%region_18.19 | all-reduce | flops 8192 | bytes 65536 | tf_op jit(solution)/shard_map/psum | solution.py:42
  695.2 66.8 %all-gather.6.cloned.1.call-done = bf16[4,640,1152]{2,0,1:T(4,128)(2,1)} async-done(((bf16[4,160,1152]{2,0,1:T(4,128)(2,1)}), bf16[4,640,1152]{2,0,1:T(4,128)(2,1)}) %all-gather.6.cloned.1.call-update) | async-done | bytes 5898256 | tf_op jit(solution)/shard_map/all_gather | solution.py:136
  761.9 25.5 %fusion.110 = (bf16[4,640,1024]{2,0,1:T(4,128)(2,1)S(1)}, bf16[4,640,1024]{2,0,1:T(4,128)(2,1)S(1)}, bf16[4,640,1024]{2,0,1:T(4,128)(2,1)S(1)}, bf16[4,640,1024]{2,0,1:T(4,128)(2,1)S(1)}, bf16[4,640,1024]{2,0,1:T(4,128)(2,1)}) fusion(bf16[4,640,1152]{2,0,1:T(4,128)(2,1)} %all-gather.6.cloned.1.call-done), kind=kLoop, calls=%fused_computation.198 | loop fusion | bytes 52428800 | tf_op jit(solution)/shard_map/slice | solution.py:71
  813.0 18.1 %multiply_reduce_fusion.2 = (f32[160]{0:T(256)S(1)}, f32[4,1024]{1,0:T(4,128)S(1)}, f32[4,1024]{1,0:T(4,128)S(1)}, f32[160]{0:T(256)S(1)}, f32[4,160,1024]{2,1,0:T(8,128)}) fusion(f32[4,1024]{1,0:T(4,128)S(1)} %get-tuple-element.127, f32[4,1024]{1,0:T(4,128)S(1)} %get-tuple-element.126, f32[160]{0:T(256)S(1)} %copy-done.24, ...), kind=kOutput, calls=%fused_computation.96 | convolution fusion | flops 4248690176 | bytes 32550016 | tf_op jit(solution)/shard_map/sml,mc->scl/dot_general | solution.py:141
  831.1 15.4 %all-reduce.4 = (f32[4,1,1024]{2,0,1:T(4,128)S(1)}, f32[4,1,1024]{2,0,1:T(4,128)S(1)}) all-reduce(f32[4,1,1024]{2,0,1:T(4,128)S(1)} %bitcast.204, f32[4,1,1024]{2,0,1:T(4,128)S(1)} %bitcast.205), channel_id=1, replica_groups=mesh['batch'=4,'seq'=2,'ch'=4] {'ch'}, use_global_device_ids=true, to_apply=%region_22.23 | all-reduce | flops 8192 | bytes 65536 | tf_op jit(solution)/shard_map/psum | solution.py:42
  862.4 10.9 fusion.74
  873.3 41.7 %all-gather.8.cloned.1.call-done = bf16[4,640,1024]{2,0,1:T(4,128)(2,1)} async-done(((bf16[4,160,1024]{2,0,1:T(4,128)(2,1)}), bf16[4,640,1024]{2,0,1:T(4,128)(2,1)}) %all-gather.8.cloned.1.call-update) | async-done | bytes 5242896 | tf_op jit(solution)/shard_map/all_gather | solution.py:155
  924.1 10.0 convolution_bitcast_fusion
  934.2 25.5 %copy.67 = f32[4,1280,1024]{2,0,1:T(4,128)} copy(f32[4,1280,1024]{1,2,0:T(8,128)} %convolution_bitcast_fusion) | data formatting | bytes 41943040 | tf_op jit(solution)/shard_map/shl,hd->sdl/transpose | solution.py:119
  961.1 12.2 fusion.17
  973.3 16.3 %all-reduce.3 = (f32[4,1,1024]{2,0,1:T(4,128)S(1)}, f32[4,1,1024]{2,0,1:T(4,128)S(1)}) all-reduce(f32[4,1,1024]{2,0,1:T(4,128)S(1)} %bitcast.200, f32[4,1,1024]{2,0,1:T(4,128)S(1)} %bitcast.201), channel_id=1, replica_groups=mesh['batch'=4,'seq'=2,'ch'=4] {'ch'}, use_global_device_ids=true, to_apply=%region_26.27 | all-reduce | flops 8192 | bytes 65536 | tf_op jit(solution)/shard_map/psum | solution.py:42
  989.7 346.0 %all-reduce.23.cloned.1.call-done = f32[4,1280,1024]{2,0,1:T(4,128)} async-done(((f32[4,1280,1024]{2,0,1:T(4,128)}), f32[4,1280,1024]{2,0,1:T(4,128)}) %all-reduce.23.cloned.1.call-update) | async-done | bytes 20971536
  1351.6 20.4 %all-reduce.9 = (f32[320]{0:T(512)}, f32[320]{0:T(512)}, f32[160]{0:T(256)}, f32[160]{0:T(256)}, f32[160]{0:T(256)}, /*index=5*/f32[160]{0:T(256)}, f32[160]{0:T(256)}, f32[160]{0:T(256)}, f32[320]{0:T(512)}) all-reduce(f32[320]{0:T(512)S(1)} %get-tuple-element.84, ...), channel_id=1, replica_groups=mesh['batch'=4,'seq'=2,'ch'=4] {'batch'}, use_global_device_ids=true, to_apply=%region_29.30 | all-reduce | flops 1920 | bytes 15360 | tf_op jit(solution)/shard_map/psum | solution.py:14
  1372.0 106.8 %all-reduce.25.cloned.1.call-done = (f32[320,640]{1,0:T(8,128)}, f32[5,160,640]{2,1,0:T(8,128)}, f32[160,1280]{1,0:T(8,128)}) async-done(((f32[320,640]{1,0:T(8,128)}, f32[5,160,640]{2,1,0:T(8,128)}, f32[160,1280]{1,0:T(8,128)}), (f32[320,640]{1,0:T(8,128)}, f32[5,160,640]{2,1,0:T(8,128)}, f32[160,1280]{1,0:T(8,128)})) %all-reduce.25.cloned.1.call-update) | async-done | bytes 3686416 | tf_op jit(solution)/shard_map/psum | solution.py:14
  (162 shorter events, 160.0 us)
Async XLA Ops:
  7.2 306.9 %copy-start = (bf16[5,160,640]{2,1,0:T(8,128)(2,1)S(1)}, bf16[5,160,640]{2,1,0:T(8,128)(2,1)}, u32[]{:S(2)}) copy-start(bf16[5,160,640]{2,1,0:T(8,128)(2,1)} %param.23) | copy-start | bytes 3072004
  7.2 20.4 %copy-start.28 = (f32[320]{0:T(512)S(1)}, f32[320]{0:T(512)}, u32[]{:S(2)}) copy-start(f32[320]{0:T(512)} %param.17) | copy-start | bytes 3844
  7.2 20.4 %copy-start.34 = (f32[320]{0:T(512)S(1)}, f32[320]{0:T(512)}, u32[]{:S(2)}) copy-start(f32[320]{0:T(512)} %param.18) | copy-start | bytes 3844
  7.2 261.0 %all-reduce.19.cloned.1.call-start = ((), (), s32[]{:S(2)}) async-start(), calls=%async_computation.3 | async-start | bytes 20971520
  62.4 480.5 %all-reduce.21.cloned.1.call-start = ((), (), s32[]{:S(2)}) async-start(), calls=%async_computation.4 | async-start | bytes 20971520
  63.2 235.7 %collective-permute-start.2 = (s32[4,64]{1,0:T(4,128)S(1)}, s32[4,64]{1,0:T(4,128)S(1)}, u32[]{:S(2)}, u32[]{:S(2)}) collective-permute-start(s32[4,64]{1,0:T(4,128)S(1)} %get-tuple-element.124), channel_id=1, source_target_pairs={{4,0},{5,1},{6,2},{7,3},{12,8},{13,9},{14,10},{15,11},{20,16},{21,... | collective-permute-start | bytes 3080 | tf_op jit(solution)/shard_map/ppermute | solution.py:28
  64.5 234.4 %collective-permute-start = (s32[4,64]{1,0:T(4,128)S(1)}, s32[4,64]{1,0:T(4,128)S(1)}, u32[]{:S(2)}, u32[]{:S(2)}) collective-permute-start(s32[4,64]{1,0:T(4,128)S(1)} %get-tuple-element.125), channel_id=1, source_target_pairs={{0,4},{1,5},{2,6},{3,7},{8,12},{9,13},{10,14},{11,15},{16,20},{17,... | collective-permute-start | bytes 3080 | tf_op jit(solution)/shard_map/ppermute | solution.py:27
  68.8 203.3 %copy-start.23 = (f32[160]{0:T(256)S(1)}, f32[160]{0:T(256)}, u32[]{:S(2)}) copy-start(f32[160]{0:T(256)} %param.20) | copy-start | bytes 1924
  272.0 17.2 %copy-start.32 = (f32[160]{0:T(256)S(1)}, f32[160]{0:T(256)}, u32[]{:S(2)}) copy-start(f32[160]{0:T(256)} %param.22) | copy-start | bytes 1924
  297.6 3.2 collective-permute-start.1
  299.0 10.7 collective-permute-start.3
  336.1 314.4 %all-gather.4.cloned.1.call-start = ((), (), s32[]{:S(2)}) async-start(), calls=%async_computation | async-start | bytes 13107200 | tf_op jit(solution)/shard_map/all_gather | solution.py:122
  336.8 209.9 %copy-start.25 = (f32[160]{0:T(256)S(1)}, f32[160]{0:T(256)}, u32[]{:S(2)}) copy-start(f32[160]{0:T(256)} %param.24) | copy-start | bytes 1924
  336.8 425.1 %all-gather.6.cloned.1.call-start = ((), (), s32[]{:S(2)}) async-start(), calls=%async_computation.1 | async-start | bytes 7372800 | tf_op jit(solution)/shard_map/all_gather | solution.py:136
  546.8 17.9 %copy-start.30 = (f32[160]{0:T(256)S(1)}, f32[160]{0:T(256)}, u32[]{:S(2)}) copy-start(f32[160]{0:T(256)} %param.25) | copy-start | bytes 1924
  546.8 17.9 %copy-start.37 = (f32[160]{0:T(256)S(1)}, f32[160]{0:T(256)}, u32[]{:S(2)}) copy-start(f32[160]{0:T(256)} %param.26) | copy-start | bytes 1924
  564.7 85.9 %copy-start.13 = (bf16[160,1280]{1,0:T(8,128)(2,1)S(1)}, bf16[160,1280]{1,0:T(8,128)(2,1)}, u32[]{:S(2)}) copy-start(bf16[160,1280]{1,0:T(8,128)(2,1)} %param.27) | copy-start | bytes 1228804
  683.8 4.4 collective-permute-start.5
  685.1 4.1 collective-permute-start.4
  694.9 220.1 %all-gather.8.cloned.1.call-start = ((), (), s32[]{:S(2)}) async-start(), calls=%async_computation.2 | async-start | bytes 6553600 | tf_op jit(solution)/shard_map/all_gather | solution.py:155
  853.5 106.5 %all-reduce.27.cloned.1.call-start = ((), (), s32[]{:S(2)}) async-start(), calls=%async_computation.7 | async-start | bytes 7372800 | tf_op jit(solution)/shard_map/psum | solution.py:13
  923.2 412.5 %all-reduce.23.cloned.1.call-start = ((), (), s32[]{:S(2)}) async-start(), calls=%async_computation.5 | async-start | bytes 41943040
  959.7 519.1 %all-reduce.25.cloned.1.call-start = ((), (), s32[]{:S(2)}) async-start(), calls=%async_computation.6 | async-start | bytes 7372800 | tf_op jit(solution)/shard_map/psum | solution.py:14
  989.7 349.9 %copy-start.36 = (f32[320]{0:T(512)S(1)}, f32[320]{0:T(512)}, u32[]{:S(2)}) copy-start(f32[320]{0:T(512)} %param.28) | copy-start | bytes 3844
  (33 other events, 183.8 us)
Sparse Core Ops, SparseCore 0:
  62.5 205.6 all-reduce.18
  336.2 206.7 all-reduce.20
  544.8 105.6 all-gather.3
  695.0 66.8 all-gather.5
  853.6 61.4 all-gather.7
  923.3 24.4 all-reduce.26
  959.8 375.8 all-reduce.22
  1338.3 140.5 all-reduce.24
